TPU v7x, 512 devices: a whole 4x8x8 slice. The times are simulated.
512 devices in a mesh: rep: 4 (over z_lo), fsdp: 16 (over y, core), tp: 8 (over z_hi, x).
Axes of the slice: x: 4, y: 8, z: 8 (z_hi: 2, z_lo: 4; z = z_hi * 4 + z_lo), core: 2. Of those that a mesh axis runs over, the one named last changes fastest.
Arguments:
- delta_attn: float32 [4, 4, 768, 768], P('rep', None, 'fsdp', 'tp'), may hold values from -4 to 4
- delta_in: float32 [4, 768, 3072], P('rep', 'fsdp', 'tp'), may hold values from -4 to 4
- delta_out: float32 [4, 3072, 768], P('rep', 'fsdp', 'tp'), may hold values from -4 to 4
- delta_small: float32 [4, 1920], P('rep'), may hold values from -4 to 4
- emb_left: float32 [4, 8, 4016, 64], P('rep', 'tp', 'fsdp'), may hold values from -6 to 6
- emb_right: float32 [4, 64, 768], P('rep'), may hold values from -0.75 to 0.75
- anchor_attn: float32 [8, 294912], P('tp', 'fsdp'), may hold values from -6 to 6
- anchor_in: float32 [8, 294912], P('tp', 'fsdp'), may hold values from -6 to 6
- anchor_out: float32 [8, 294912], P('tp', 'fsdp'), may hold values from -6 to 6
- anchor_small: float32 [1920], P('fsdp'), may hold values from -6 to 6
- anchor_emb: float32 [8, 16, 4, 48192], P('tp', 'fsdp', 'rep'), may hold values from -6 to 6
- moment_attn: float32 [8, 294912], P('tp', 'fsdp'), may hold values from -4 to 4
- moment_in: float32 [8, 294912], P('tp', 'fsdp'), may hold values from -4 to 4
- moment_out: float32 [8, 294912], P('tp', 'fsdp'), may hold values from -4 to 4
- moment_small: float32 [1920], P('fsdp'), may hold values from -4 to 4
- moment_emb: float32 [8, 16, 4, 48192], P('tp', 'fsdp', 'rep'), may hold values from -4 to 4
Outputs:
- new_attn: float32 [4, 768, 768], P(None, 'fsdp', 'tp')
- new_in: float32 [768, 3072], P('fsdp', 'tp')
- new_out: float32 [3072, 768], P('fsdp', 'tp')
- new_small: float32 [1920], replicated
- new_emb: float32 [32128, 768], P('tp', 'fsdp')
- next_attn: float32 [8, 294912], P('tp', 'fsdp')
- next_in: float32 [8, 294912], P('tp', 'fsdp')
- next_out: float32 [8, 294912], P('tp', 'fsdp')
- next_small: float32 [1920], P('fsdp')
- next_emb: float32 [8, 16, 4, 48192], P('tp', 'fsdp', 'rep')
All inputs are finite; a program needn't handle non-finite values.
Results may differ from a plain program's by a relative error of at most 0.000071.
Values sent between devices are 32-bit elements; how exact they have to be, the bound alone decides.
A program may use at most 64 MiB of HBM per device.

v0:
```python
import jax
import jax.numpy as jnp
from jax import lax
from jax.sharding import PartitionSpec as P

OUTER_RATE = 0.7
MOMENTUM_COEF = 0.9


def nesterov(anchor, moment, mean_delta):
    moment_next = MOMENTUM_COEF * moment + mean_delta
    updated = anchor - OUTER_RATE * (mean_delta + MOMENTUM_COEF * moment_next)
    return (updated, moment_next)


def to_blocks(matrix, lead, shards):
    local_rows = matrix.shape[-2]
    width = matrix.shape[-1] // shards
    shaped = matrix.reshape(lead, local_rows, shards, width)
    return jnp.transpose(shaped, (2, 3, 0, 1))


def from_blocks(blocks):
    shards, width, lead, local_rows = blocks.shape
    return jnp.transpose(blocks, (2, 3, 0, 1)).reshape(lead, local_rows, shards * width)


def on_device(
    delta_attn,
    delta_in,
    delta_out,
    delta_small,
    emb_left,
    emb_right,
    anchor_attn,
    anchor_in,
    anchor_out,
    anchor_small,
    anchor_emb,
    moment_attn,
    moment_in,
    moment_out,
    moment_small,
    moment_emb,
):
    groups = lax.axis_size("rep")
    shards = lax.axis_size("fsdp")
    send_attn = to_blocks(delta_attn[0], 4, shards)
    send_in = to_blocks(delta_in[0][None], 1, shards)
    send_out = to_blocks(delta_out[0][None], 1, shards)
    flat_attn, flat_in, flat_out = (
        lax.all_to_all(send_attn, "fsdp", split_axis=0, concat_axis=3, tiled=True),
        lax.all_to_all(send_in, "fsdp", split_axis=0, concat_axis=3, tiled=True),
        lax.all_to_all(send_out, "fsdp", split_axis=0, concat_axis=3, tiled=True),
    )
    block_shapes = (flat_attn.shape, flat_in.shape, flat_out.shape)
    portion = anchor_small.shape[0]
    small_local = lax.dynamic_slice_in_dim(
        delta_small[0], lax.axis_index("fsdp") * portion, portion, 0
    )[None, :]
    differences = (
        flat_attn.reshape(flat_attn.shape[1] * flat_attn.shape[2], flat_attn.shape[3]),
        flat_in.reshape(flat_in.shape[1], flat_in.shape[3]),
        flat_out.reshape(flat_out.shape[1], flat_out.shape[3]),
        small_local,
    )
    anchors = (
        anchor_attn.reshape(differences[0].shape),
        anchor_in.reshape(differences[1].shape),
        anchor_out.reshape(differences[2].shape),
        anchor_small[None, :],
    )
    moments = (
        moment_attn.reshape(differences[0].shape),
        moment_in.reshape(differences[1].shape),
        moment_out.reshape(differences[2].shape),
        moment_small[None, :],
    )
    totals = lax.psum((differences[0], differences[1], differences[2], differences[3]), "rep")
    updated_list = []
    moment_list = []
    for summed, anchor_part, moment_part in zip(totals, anchors, moments):
        updated, moment_next = nesterov(anchor_part, moment_part, summed / groups)
        updated_list.append(updated)
        moment_list.append(moment_next)
    back_attn = updated_list[0].reshape(block_shapes[0])
    back_in = updated_list[1].reshape(block_shapes[1])
    back_out = updated_list[2].reshape(block_shapes[2])
    train_attn, train_in, train_out = (
        lax.all_to_all(back_attn, "fsdp", split_axis=3, concat_axis=0, tiled=True),
        lax.all_to_all(back_in, "fsdp", split_axis=3, concat_axis=0, tiled=True),
        lax.all_to_all(back_out, "fsdp", split_axis=3, concat_axis=0, tiled=True),
    )
    new_attn = from_blocks(train_attn)
    new_in = from_blocks(train_in)[0]
    new_out = from_blocks(train_out)[0]
    new_small = lax.all_gather(updated_list[3].reshape(portion), "fsdp", axis=0, tiled=True)
    left_local = emb_left[0, 0]
    right_local = emb_right[0]
    block_rows = left_local.shape[0]
    column_count = right_local.shape[1] // groups
    product_term = jnp.dot(
        left_local, right_local, precision=lax.Precision.HIGHEST, preferred_element_type=jnp.float32
    )
    summed_emb = lax.psum_scatter(product_term, "rep", scatter_dimension=1, tiled=True)
    anchor_rows = anchor_emb[0, 0, 0].reshape(block_rows, column_count)
    moment_rows = moment_emb[0, 0, 0].reshape(block_rows, column_count)
    new_emb_part, next_emb_part = nesterov(anchor_rows, moment_rows, summed_emb / groups)
    full_rows = lax.all_gather(new_emb_part, "rep", axis=1, tiled=True)
    new_emb = lax.all_to_all(full_rows, "fsdp", split_axis=1, concat_axis=0, tiled=True)
    return (
        new_attn,
        new_in,
        new_out,
        new_small,
        new_emb,
        moment_list[0].reshape(moment_attn.shape),
        moment_list[1].reshape(moment_in.shape),
        moment_list[2].reshape(moment_out.shape),
        moment_list[3].reshape(moment_small.shape),
        next_emb_part.reshape(moment_emb.shape),
    )


def solution(mesh):
    placed = (
        P("rep", None, "fsdp", "tp"),
        P("rep", "fsdp", "tp"),
        P("rep", "fsdp", "tp"),
        P("rep", None),
        P("rep", "tp", "fsdp", None),
        P("rep", None, None),
        P("tp", "fsdp"),
        P("tp", "fsdp"),
        P("tp", "fsdp"),
        P("fsdp"),
        P("tp", "fsdp", "rep", None),
        P("tp", "fsdp"),
        P("tp", "fsdp"),
        P("tp", "fsdp"),
        P("fsdp"),
        P("tp", "fsdp", "rep", None),
    )
    return jax.shard_map(
        on_device,
        mesh=mesh,
        in_specs=placed,
        out_specs=(
            P(None, "fsdp", "tp"),
            P("fsdp", "tp"),
            P("fsdp", "tp"),
            P(),
            P("tp", "fsdp"),
            P("tp", "fsdp"),
            P("tp", "fsdp"),
            P("tp", "fsdp"),
            P("fsdp"),
            P("tp", "fsdp", "rep", None),
        ),
        check_vma=False,
    )
```

profile of v0, /device:TPU:32, one launch (start us, length us, event | category | flops | bytes accessed | tf_op | source)
XLA Modules:
  0.0 245.8 jit_solution(11660199578842059813)
XLA Ops:
  7.2 1.1 copy.88
  9.1 8.8 %all-to-all-start.2 = ((f32[16,1,1152]{2,1,0:T(1,128)}), f32[16,1,1152]{2,1,0:T(1,128)S(1)}, u32[]{:S(2)}, u32[]{:S(2)}) async-start(f32[16,1,1152]{2,1,0:T(1,128)} %reshape.155), calls=%async_computation.2 | async-start | bytes 147456 | tf_op jit(solution)/shard_map/all_to_all | solution.py:53
  17.9 1.0 copy.83
  18.9 0.9 reshape.151
  19.8 1.4 all-to-all-done.2
  21.2 8.2 %all-to-all-start = ((f32[16,1,1152]{2,1,0:T(1,128)}), f32[16,1,1152]{2,1,0:T(1,128)S(1)}, u32[]{:S(2)}, u32[]{:S(2)}) async-start(f32[16,1,1152]{2,1,0:T(1,128)} %reshape.151), calls=%async_computation | async-start | bytes 147456 | tf_op jit(solution)/shard_map/all_to_all | solution.py:52
  29.3 1.6 copy.94
  32.6 8.2 %all-to-all-start.4 = ((f32[16,6,1,192]{3,2,1,0:T(1,128)}), f32[16,6,1,192]{3,2,1,0:T(1,128)S(1)}, u32[]{:S(2)}, u32[]{:S(2)}) async-start(f32[16,6,1,192]{3,2,1,0:T(1,128)} %bitcast.21), calls=%async_computation.4 | async-start | bytes 196608 | tf_op jit(solution)/shard_map/all_to_all | solution.py:54
  43.5 1.1 all-to-all-done.4
  45.6 1.7 fusion
  55.9 48.3 %all-reduce.4.cloned.1.call-done = (f32[24,768]{1,0:T(8,128)}, f32[24,768]{1,0:T(8,128)}, f32[6,3072]{1,0:T(8,128)}) async-done(((f32[24,768]{1,0:T(8,128)}, f32[24,768]{1,0:T(8,128)}, f32[6,3072]{1,0:T(8,128)}), (f32[24,768]{1,0:T(8,128)}, f32[24,768]{1,0:T(8,128)}, f32[6,3072]{1,0:T(8,128)})) %all-reduce.4.cloned.1.call-update) | async-done | bytes 221200 | tf_op jit(solution)/shard_map/psum | solution.py:79
  104.1 1.6 fusion.2
  105.7 1.6 copy.96
  107.3 13.7 %reduce.32 = f32[3072,6]{1,0:T(8,128)S(1)} reduce(f32[3072,1,1,6]{3,2,1,0:T(1,128)S(1)} %bitcast.106, f32[]{:T(128)} %broadcast.90), dimensions={1,2}, to_apply=%bitcast.99.reduce_sub_computation | reduce | bytes 147460
  121.1 1.9 reshape.159
  123.0 7.2 %all-to-all-start.5 = ((f32[16,1,1152]{2,1,0:T(1,128)}), f32[16,1,1152]{2,1,0:T(1,128)S(1)}, u32[]{:S(2)}, u32[]{:S(2)}) async-start(f32[16,1,1152]{2,1,0:T(1,128)} %reshape.159), calls=%async_computation.5 | async-start | bytes 147456 | tf_op jit(solution)/shard_map/all_to_all | solution.py:92
  131.2 1.6 reduce.30
  132.8 0.9 reshape.157
  135.1 2.5 %reshape.153 = f32[16,1,1152]{2,1,0:T(1,128)} reshape(f32[768,1,4,6]{3,2,1,0:T(4,128)S(1)} %bitcast.103) | data formatting | bytes 147456
  137.6 7.2 %all-to-all-start.3 = ((f32[16,1,1152]{2,1,0:T(1,128)}), f32[16,1,1152]{2,1,0:T(1,128)S(1)}, u32[]{:S(2)}, u32[]{:S(2)}) async-start(f32[16,1,1152]{2,1,0:T(1,128)} %reshape.157), calls=%async_computation.3 | async-start | bytes 147456 | tf_op jit(solution)/shard_map/all_to_all | solution.py:91
  144.9 1.0 multiply_add_fusion
  145.9 2.2 all-to-all-done.3
  148.1 8.1 %all-to-all-start.1 = ((f32[16,1,1152]{2,1,0:T(1,128)}), f32[16,1,1152]{2,1,0:T(1,128)S(1)}, u32[]{:S(2)}, u32[]{:S(2)}) async-start(f32[16,1,1152]{2,1,0:T(1,128)} %reshape.153), calls=%async_computation.1 | async-start | bytes 147456 | tf_op jit(solution)/shard_map/all_to_all | solution.py:90
  156.3 18.3 %all_gather.7 = f32[251,768]{0,1:T(8,128)} all-gather(f32[251,192]{0,1:T(8,128)S(1)} %get-tuple-element.54), channel_id=1, replica_groups=mesh['rep'=4,'fsdp'=16,'tp'=8] {'rep'}, dimensions={1}, use_global_device_ids=true | all-gather | bytes 963840 | tf_op jit(solution)/shard_map/all_gather | solution.py:109
  174.6 7.2 %all-to-all-start.6 = ((f32[251,16,48]{0,2,1:T(8,128)}), f32[251,16,48]{0,2,1:T(8,128)S(1)}, u32[]{:S(2)}, u32[]{:S(2)}) async-start(f32[251,16,48]{0,2,1:T(8,128)} %bitcast.35), calls=%async_computation.7 | async-start | bytes 1572864 | tf_op jit(solution)/shard_map/all_to_all | solution.py:110
  181.8 1.3 dynamic-slice.1
  184.5 10.2 %psum.31 = f32[1,120]{1,0:T(1,128)S(1)} all-reduce(f32[1,120]{1,0:T(1,128)S(1)} %constant_dynamic-slice_fusion), channel_id=1, replica_groups=mesh['rep'=4,'fsdp'=16,'tp'=8] {'rep'}, use_global_device_ids=true, to_apply=%region_3.0 | all-reduce | flops 120 | bytes 960 | tf_op jit(solution)/shard_map/psum | solution.py:79
  194.8 26.9 %all-reduce = f32[1920]{0:T(1024)} all-reduce(f32[1920]{0:T(1024)S(1)} %bitcast_dynamic-update-slice_fusion), channel_id=2, replica_groups=mesh['rep'=4,'fsdp'=16,'tp'=8] {'fsdp'}, use_global_device_ids=true, to_apply=%add | all-reduce | flops 1920 | bytes 15360 | tf_op jit(solution)/shard_map/all_gather | solution.py:97
  225.2 2.5 reshape.160
  232.5 2.0 reshape.154
  236.3 0.9 reshape.103
  237.7 1.3 all_to_all.110
  (116 shorter events, 28.3 us)
Async XLA Ops:
  7.2 38.4 %copy-start = (f32[1,64,768]{2,1,0:T(8,128)S(1)}, f32[1,64,768]{2,1,0:T(8,128)}, u32[]{:S(2)}) copy-start(f32[1,64,768]{2,1,0:T(8,128)} %param.21) | copy-start | bytes 589828
  9.1 12.1 %all-to-all-start.2 = ((f32[16,1,1152]{2,1,0:T(1,128)}), f32[16,1,1152]{2,1,0:T(1,128)S(1)}, u32[]{:S(2)}, u32[]{:S(2)}) async-start(f32[16,1,1152]{2,1,0:T(1,128)} %reshape.155), calls=%async_computation.2 | async-start | bytes 147456 | tf_op jit(solution)/shard_map/all_to_all | solution.py:53
  21.2 11.4 %all-to-all-start = ((f32[16,1,1152]{2,1,0:T(1,128)}), f32[16,1,1152]{2,1,0:T(1,128)S(1)}, u32[]{:S(2)}, u32[]{:S(2)}) async-start(f32[16,1,1152]{2,1,0:T(1,128)} %reshape.151), calls=%async_computation | async-start | bytes 147456 | tf_op jit(solution)/shard_map/all_to_all | solution.py:52
  32.3 13.3 %copy-start.21 = (f32[1,1,251,64]{2,3,1,0:T(8,128)S(1)}, f32[1,1,251,64]{2,3,1,0:T(8,128)}, u32[]{:S(2)}) copy-start(f32[1,1,251,64]{2,3,1,0:T(8,128)} %param.20) | copy-start | bytes 192772
  32.6 12.0 %all-to-all-start.4 = ((f32[16,6,1,192]{3,2,1,0:T(1,128)}), f32[16,6,1,192]{3,2,1,0:T(1,128)S(1)}, u32[]{:S(2)}, u32[]{:S(2)}) async-start(f32[16,6,1,192]{3,2,1,0:T(1,128)} %bitcast.21), calls=%async_computation.4 | async-start | bytes 196608 | tf_op jit(solution)/shard_map/all_to_all | solution.py:54
  40.8 63.4 %all-reduce.4.cloned.1.call-start = ((), (), s32[]{:S(2)}) async-start(), calls=%async_computation.9 | async-start | bytes 491520 | tf_op jit(solution)/shard_map/psum | solution.py:79
  42.7 5.2 %copy-start.13 = (f32[1,18432]{1,0:T(1,128)S(1)}, f32[1,18432]{1,0:T(1,128)}, u32[]{:S(2)}) copy-start(f32[1,18432]{1,0:T(1,128)} %param.24) | copy-start | bytes 221188
  42.7 6.0 %copy-start.17 = (f32[1,18432]{1,0:T(1,128)S(1)}, f32[1,18432]{1,0:T(1,128)}, u32[]{:S(2)}) copy-start(f32[1,18432]{1,0:T(1,128)} %param.29) | copy-start | bytes 221188
  42.7 6.0 %copy-start.18 = (f32[1,18432]{1,0:T(1,128)S(1)}, f32[1,18432]{1,0:T(1,128)}, u32[]{:S(2)}) copy-start(f32[1,18432]{1,0:T(1,128)} %param.28) | copy-start | bytes 221188
  44.6 4.7 %copy-start.14 = (f32[1,18432]{1,0:T(1,128)S(1)}, f32[1,18432]{1,0:T(1,128)}, u32[]{:S(2)}) copy-start(f32[1,18432]{1,0:T(1,128)} %param.23) | copy-start | bytes 221188
  45.3 6.0 %copy-start.15 = (f32[1,18432]{1,0:T(1,128)S(1)}, f32[1,18432]{1,0:T(1,128)}, u32[]{:S(2)}) copy-start(f32[1,18432]{1,0:T(1,128)} %param.22) | copy-start | bytes 221188
  45.4 7.5 %copy-start.16 = (f32[1,18432]{1,0:T(1,128)S(1)}, f32[1,18432]{1,0:T(1,128)}, u32[]{:S(2)}) copy-start(f32[1,18432]{1,0:T(1,128)} %param.27) | copy-start | bytes 221188
  45.4 8.3 %copy-start.11 = (f32[1,1,1,48192]{3,2,1,0:T(1,128)S(1)}, f32[1,1,1,48192]{3,2,1,0:T(1,128)}, u32[]{:S(2)}) copy-start(f32[1,1,1,48192]{3,2,1,0:T(1,128)} %param.26) | copy-start | bytes 578308
  45.4 99.5 %reduce-scatter.2.cloned.1.call-start = ((), (), s32[]{:S(2)}) async-start(), calls=%async_computation.8 | async-start | bytes 983040 | tf_op jit(solution)/shard_map/reduce_scatter | solution.py:105
  47.4 7.0 %copy-start.12 = (f32[1,1,1,48192]{3,2,1,0:T(1,128)S(1)}, f32[1,1,1,48192]{3,2,1,0:T(1,128)}, u32[]{:S(2)}) copy-start(f32[1,1,1,48192]{3,2,1,0:T(1,128)} %param.31) | copy-start | bytes 578308
  121.0 9.2 %copy-start.9 = (f32[24,768]{1,0:T(8,128)S(1)}, f32[24,768]{1,0:T(8,128)}, u32[]{:S(2)}) copy-start(f32[24,768]{1,0:T(8,128)} %reshape.92) | copy-start | bytes 221188
  121.0 9.2 %copy-start.10 = (f32[24,768]{1,0:T(8,128)S(1)}, f32[24,768]{1,0:T(8,128)}, u32[]{:S(2)}) copy-start(f32[24,768]{1,0:T(8,128)} %mul.77) | copy-start | bytes 221188
  121.0 9.2 %copy-start.20 = (f32[24,768]{1,0:T(8,128)S(1)}, f32[24,768]{1,0:T(8,128)}, u32[]{:S(2)}) copy-start(f32[24,768]{1,0:T(8,128)} %get-tuple-element.51) | copy-start | bytes 221188
  121.0 12.7 %copy-start.7 = (f32[24,768]{1,0:T(8,128)S(1)}, f32[24,768]{1,0:T(8,128)}, u32[]{:S(2)}) copy-start(f32[24,768]{1,0:T(8,128)} %reshape.88) | copy-start | bytes 221188
  121.0 12.7 %copy-start.8 = (f32[24,768]{1,0:T(8,128)S(1)}, f32[24,768]{1,0:T(8,128)}, u32[]{:S(2)}) copy-start(f32[24,768]{1,0:T(8,128)} %mul.73) | copy-start | bytes 221188
  121.0 12.7 %copy-start.19 = (f32[24,768]{1,0:T(8,128)S(1)}, f32[24,768]{1,0:T(8,128)}, u32[]{:S(2)}) copy-start(f32[24,768]{1,0:T(8,128)} %get-tuple-element.50) | copy-start | bytes 221188
  123.0 14.6 %all-to-all-start.5 = ((f32[16,1,1152]{2,1,0:T(1,128)}), f32[16,1,1152]{2,1,0:T(1,128)S(1)}, u32[]{:S(2)}, u32[]{:S(2)}) async-start(f32[16,1,1152]{2,1,0:T(1,128)} %reshape.159), calls=%async_computation.5 | async-start | bytes 147456 | tf_op jit(solution)/shard_map/all_to_all | solution.py:92
  134.4 10.5 %copy-start.1 = (f32[251,192]{0,1:T(8,128)S(1)}, f32[251,192]{0,1:T(8,128)}, u32[]{:S(2)}) copy-start(f32[251,192]{0,1:T(8,128)} %copy.99) | copy-start | bytes 578308
  137.6 10.5 %all-to-all-start.3 = ((f32[16,1,1152]{2,1,0:T(1,128)}), f32[16,1,1152]{2,1,0:T(1,128)S(1)}, u32[]{:S(2)}, u32[]{:S(2)}) async-start(f32[16,1,1152]{2,1,0:T(1,128)} %reshape.157), calls=%async_computation.3 | async-start | bytes 147456 | tf_op jit(solution)/shard_map/all_to_all | solution.py:91
  145.8 48.8 %copy-start.22 = (f32[120]{0:T(128)S(1)}, f32[120]{0:T(128)}, u32[]{:S(2)}) copy-start(f32[120]{0:T(128)} %param.25) | copy-start | bytes 1444
  145.9 48.8 %copy-start.23 = (f32[120]{0:T(128)S(1)}, f32[120]{0:T(128)}, u32[]{:S(2)}) copy-start(f32[120]{0:T(128)} %param.30) | copy-start | bytes 1444
  145.9 76.3 %copy-start.2 = (f32[1,1,6,3072]{3,2,1,0:T(8,128)S(1)}, f32[1,1,6,3072]{3,2,1,0:T(8,128)}, u32[]{:S(2)}) copy-start(f32[1,1,6,3072]{3,2,1,0:T(8,128)} %get-tuple-element.55) | copy-start | bytes 221188
  145.9 77.0 %copy-start.5 = (f32[1,1,24,768]{3,2,1,0:T(8,128)S(1)}, f32[1,1,24,768]{3,2,1,0:T(8,128)}, u32[]{:S(2)}) copy-start(f32[1,1,24,768]{3,2,1,0:T(8,128)} %get-tuple-element.57) | copy-start | bytes 221188
  145.9 77.7 %copy-start.6 = (f32[1,1,24,768]{3,2,1,0:T(8,128)S(1)}, f32[1,1,24,768]{3,2,1,0:T(8,128)}, u32[]{:S(2)}) copy-start(f32[1,1,24,768]{3,2,1,0:T(8,128)} %get-tuple-element.59) | copy-start | bytes 221188
  148.1 76.2 %copy-start.3 = (f32[16,1,1152]{2,1,0:T(1,128)}, f32[16,1,1152]{2,1,0:T(1,128)S(1)}, u32[]{:S(2)}) copy-start(f32[16,1,1152]{2,1,0:T(1,128)S(1)} %all-to-all-done.3) | copy-start | bytes 221188
  148.1 26.4 %all-to-all-start.1 = ((f32[16,1,1152]{2,1,0:T(1,128)}), f32[16,1,1152]{2,1,0:T(1,128)S(1)}, u32[]{:S(2)}, u32[]{:S(2)}) async-start(f32[16,1,1152]{2,1,0:T(1,128)} %reshape.153), calls=%async_computation.1 | async-start | bytes 147456 | tf_op jit(solution)/shard_map/all_to_all | solution.py:90
  174.6 62.6 %all-to-all-start.6 = ((f32[251,16,48]{0,2,1:T(8,128)}), f32[251,16,48]{0,2,1:T(8,128)S(1)}, u32[]{:S(2)}, u32[]{:S(2)}) async-start(f32[251,16,48]{0,2,1:T(8,128)} %bitcast.35), calls=%async_computation.7 | async-start | bytes 1572864 | tf_op jit(solution)/shard_map/all_to_all | solution.py:110
  (1 other events, 1.5 us)
Sparse Core Ops, SparseCore 0:
  45.5 58.6 all-reduce.3
  107.8 30.1 reduce-scatter.1
where the time goes:
time: 247 us; the launch traced here: 246 us
  blocking collectives  55.4 us (22%)
  starting transfers between devices  55.2 us (22%)
  waiting for transfers between devices  53.1 us (21%)
  local copies, waits for them, and re-layouts  37.2 us (15%)
  other arithmetic  27.9 us (11%)
  between operations  15.3 us (6%)
    psum x1, waiting for transfers between devices, on_device(): lax.psum((differences[0], differences[1], differences[2], differences[3])...  48.3 us
    all_gather x1, blocking collectives, on_device(): lax.all_gather(updated_list[3].reshape(portion), 'fsdp', axis=0, tiled=True)  26.9 us
    unnamed x70, local copies, waits for them, and re-layouts  22.5 us
    unnamed x10, other arithmetic  21.2 us
    all_gather x1, blocking collectives, on_device(): full_rows = lax.all_gather(new_emb_part, 'rep', axis=1, tiled=True)  18.3 us
    psum x1, blocking collectives, on_device(): lax.psum((differences[0], differences[1], differences[2], differences[3])...  10.2 us
    all_to_all x1, starting transfers between devices, on_device(): lax.all_to_all(send_in, 'fsdp', split_axis=0, concat_axis=3, tiled=True)  8.82 us
    all_to_all x1, starting transfers between devices, on_device(): lax.all_to_all(send_out, 'fsdp', split_axis=0, concat_axis=3, tiled=True)  8.17 us
  transfers between devices with their start and end apart: 9, of which 5 were waited for; matrix products, arithmetic and copies ran while one was open for 25% of the time, Pallas kernels for 0%

commit v1 on v0

--- a/solution.py
+++ b/solution.py
@@ -94,7 +94,23 @@
     new_attn = from_blocks(train_attn)
     new_in = from_blocks(train_in)[0]
     new_out = from_blocks(train_out)[0]
-    new_small = lax.all_gather(updated_list[3].reshape(portion), "fsdp", axis=0, tiled=True)
+
+    def _expand_corner(chunk):
+        amount_of = lax.axis_size("fsdp")
+        block_list = [(i0, (i0 + 1) % amount_of) for i0 in range(amount_of)]
+        steps_seen = [(i0, (i0 - 1) % amount_of) for i0 in range(amount_of)]
+        w_next, formed = ([chunk], [chunk])
+        for _ in range(amount_of // 2):
+            w_next.append(lax.ppermute(w_next[-1], "fsdp", block_list))
+        for _ in range((amount_of - 1) // 2):
+            formed.append(lax.ppermute(formed[-1], "fsdp", steps_seen))
+        part_next = jnp.concatenate([*w_next[::-1], *formed[1:]], axis=0)
+        taken_in = jnp.roll(
+            part_next, (lax.axis_index("fsdp") - amount_of // 2) * chunk.shape[0], axis=0
+        )
+        return taken_in
+
+    new_small = _expand_corner(updated_list[3].reshape(portion))
     left_local = emb_left[0, 0]
     right_local = emb_right[0]
     block_rows = left_local.shape[0]

time: 247 us -> 255 us (1.032)
  the two profiles are of different devices: /device:TPU:32 before, /device:TPU:2 now
where the time goes in v1:
time: 255 us; the launch traced here: 254 us
  waiting for transfers between devices  86.5 us (34%)
  starting transfers between devices  58.8 us (23%)
  local copies, waits for them, and re-layouts  36.7 us (14%)
  blocking collectives  28.5 us (11%)
  other arithmetic  27.3 us (11%)
  between operations  14.7 us (6%)
    psum x1, waiting for transfers between devices, on_device(): lax.psum((differences[0], differences[1], differences[2], differences[3])...  45.7 us
    unnamed x68, local copies, waits for them, and re-layouts  21.2 us
    unnamed x9, other arithmetic  20.9 us
    ppermute x7, starting transfers between devices, _expand_corner(): formed.append(lax.ppermute(formed[-1], 'fsdp', steps_seen))  20.3 us
    all_gather x1, blocking collectives, on_device(): full_rows = lax.all_gather(new_emb_part, 'rep', axis=1, tiled=True)  18.3 us
    ppermute x8, waiting for transfers between devices, _expand_corner(): w_next.append(lax.ppermute(w_next[-1], 'fsdp', block_list))  16.2 us
    psum x1, blocking collectives, on_device(): lax.psum((differences[0], differences[1], differences[2], differences[3])...  10.2 us
    all_to_all x1, starting transfers between devices, on_device(): lax.all_to_all(send_in, 'fsdp', split_axis=0, concat_axis=3, tiled=True)  7.21 us
  transfers between devices with their start and end apart: 24, of which 20 were waited for; matrix products, arithmetic and copies ran while one was open for 24% of the time, Pallas kernels for 0%

profile of v1, /device:TPU:2, one launch (start us, length us, event | category | flops | bytes accessed | tf_op | source)
XLA Modules:
  0.0 254.3 jit_solution(18218843272024619283)
XLA Ops:
  9.1 7.2 %all-to-all-start.2 = ((f32[16,1,1152]{2,1,0:T(1,128)}), f32[16,1,1152]{2,1,0:T(1,128)S(1)}, u32[]{:S(2)}, u32[]{:S(2)}) async-start(f32[16,1,1152]{2,1,0:T(1,128)} %reshape.148), calls=%async_computation.2 | async-start | bytes 147456 | tf_op jit(solution)/shard_map/all_to_all | solution.py:53
  18.2 6.1 %all-to-all-done.2 = f32[16,1,1152]{2,1,0:T(1,128)S(1)} async-done(((f32[16,1,1152]{2,1,0:T(1,128)}), f32[16,1,1152]{2,1,0:T(1,128)S(1)}, u32[]{:S(2)}, u32[]{:S(2)}) %all-to-all-start.2) | async-done | bytes 73760 | tf_op jit(solution)/shard_map/all_to_all | solution.py:53
  24.3 3.5 %all-to-all-start = ((f32[16,1,1152]{2,1,0:T(1,128)}), f32[16,1,1152]{2,1,0:T(1,128)S(1)}, u32[]{:S(2)}, u32[]{:S(2)}) async-start(f32[16,1,1152]{2,1,0:T(1,128)} %reshape.144), calls=%async_computation | async-start | bytes 147456 | tf_op jit(solution)/shard_map/all_to_all | solution.py:52
  27.8 1.6 copy.94
  30.8 4.9 %all-to-all-done = f32[16,1,1152]{2,1,0:T(1,128)S(1)} async-done(((f32[16,1,1152]{2,1,0:T(1,128)}), f32[16,1,1152]{2,1,0:T(1,128)S(1)}, u32[]{:S(2)}, u32[]{:S(2)}) %all-to-all-start) | async-done | bytes 73760 | tf_op jit(solution)/shard_map/all_to_all | solution.py:52
  35.7 3.5 %all-to-all-start.4 = ((f32[16,6,1,192]{3,2,1,0:T(1,128)}), f32[16,6,1,192]{3,2,1,0:T(1,128)S(1)}, u32[]{:S(2)}, u32[]{:S(2)}) async-start(f32[16,6,1,192]{3,2,1,0:T(1,128)} %bitcast.21), calls=%async_computation.4 | async-start | bytes 196608 | tf_op jit(solution)/shard_map/all_to_all | solution.py:54
  41.9 5.6 %all-to-all-done.4 = f32[16,6,1,192]{3,2,1,0:T(1,128)S(1)} async-done(((f32[16,6,1,192]{3,2,1,0:T(1,128)}), f32[16,6,1,192]{3,2,1,0:T(1,128)S(1)}, u32[]{:S(2)}, u32[]{:S(2)}) %all-to-all-start.4) | async-done | bytes 73760 | tf_op jit(solution)/shard_map/all_to_all | solution.py:54
  48.5 1.7 fusion
  58.8 45.7 %all-reduce.3.cloned.1.call-done = (f32[24,768]{1,0:T(8,128)}, f32[24,768]{1,0:T(8,128)}, f32[6,3072]{1,0:T(8,128)}) async-done(((f32[24,768]{1,0:T(8,128)}, f32[24,768]{1,0:T(8,128)}, f32[6,3072]{1,0:T(8,128)}), (f32[24,768]{1,0:T(8,128)}, f32[24,768]{1,0:T(8,128)}, f32[6,3072]{1,0:T(8,128)})) %all-reduce.3.cloned.1.call-update) | async-done | bytes 221200 | tf_op jit(solution)/shard_map/psum | solution.py:79
  104.5 1.6 fusion.2
  106.0 1.6 copy.96
  107.7 13.6 %reduce.32 = f32[3072,6]{1,0:T(8,128)S(1)} reduce(f32[3072,1,1,6]{3,2,1,0:T(1,128)S(1)} %bitcast.105, f32[]{:T(128)} %broadcast.89), dimensions={1,2}, to_apply=%bitcast.98.reduce_sub_computation | reduce | bytes 147460
  121.3 1.9 reshape.152
  123.2 6.9 %all-to-all-start.5 = ((f32[16,1,1152]{2,1,0:T(1,128)}), f32[16,1,1152]{2,1,0:T(1,128)S(1)}, u32[]{:S(2)}, u32[]{:S(2)}) async-start(f32[16,1,1152]{2,1,0:T(1,128)} %reshape.152), calls=%async_computation.5 | async-start | bytes 147456 | tf_op jit(solution)/shard_map/all_to_all | solution.py:92
  135.0 2.5 reshape.146
  138.1 6.6 %all-to-all-start.3 = ((f32[16,1,1152]{2,1,0:T(1,128)}), f32[16,1,1152]{2,1,0:T(1,128)S(1)}, u32[]{:S(2)}, u32[]{:S(2)}) async-start(f32[16,1,1152]{2,1,0:T(1,128)} %reshape.150), calls=%async_computation.3 | async-start | bytes 147456 | tf_op jit(solution)/shard_map/all_to_all | solution.py:91
  145.7 6.9 %all-to-all-done.3 = f32[16,1,1152]{2,1,0:T(1,128)S(1)} async-done(((f32[16,1,1152]{2,1,0:T(1,128)}), f32[16,1,1152]{2,1,0:T(1,128)S(1)}, u32[]{:S(2)}, u32[]{:S(2)}) %all-to-all-start.3) | async-done | bytes 73760 | tf_op jit(solution)/shard_map/all_to_all | solution.py:91
  152.6 3.5 %all-to-all-start.1 = ((f32[16,1,1152]{2,1,0:T(1,128)}), f32[16,1,1152]{2,1,0:T(1,128)S(1)}, u32[]{:S(2)}, u32[]{:S(2)}) async-start(f32[16,1,1152]{2,1,0:T(1,128)} %reshape.146), calls=%async_computation.1 | async-start | bytes 147456 | tf_op jit(solution)/shard_map/all_to_all | solution.py:90
  156.2 18.3 %all_gather.3 = f32[251,768]{0,1:T(8,128)} all-gather(f32[251,192]{0,1:T(8,128)S(1)} %get-tuple-element.54), channel_id=1, replica_groups=mesh['rep'=4,'fsdp'=16,'tp'=8] {'rep'}, dimensions={1}, use_global_device_ids=true | all-gather | bytes 963840 | tf_op jit(solution)/shard_map/all_gather | solution.py:125
  174.5 7.1 %all-to-all-start.6 = ((f32[251,16,48]{0,2,1:T(8,128)}), f32[251,16,48]{0,2,1:T(8,128)S(1)}, u32[]{:S(2)}, u32[]{:S(2)}) async-start(f32[251,16,48]{0,2,1:T(8,128)} %bitcast.34), calls=%async_computation.7 | async-start | bytes 1572864 | tf_op jit(solution)/shard_map/all_to_all | solution.py:126
  182.4 10.2 %psum.31 = f32[1,120]{1,0:T(1,128)S(1)} all-reduce(f32[1,120]{1,0:T(1,128)S(1)} %constant_dynamic-slice_fusion), channel_id=1, replica_groups=mesh['rep'=4,'fsdp'=16,'tp'=8] {'rep'}, use_global_device_ids=true, to_apply=%region_3.0 | all-reduce | flops 120 | bytes 960 | tf_op jit(solution)/shard_map/psum | solution.py:79
  193.1 3.0 %collective-permute-start.8 = (f32[120]{0:T(128)S(1)}, f32[120]{0:T(128)S(1)}, u32[]{:S(2)}, u32[]{:S(2)}) collective-permute-start(f32[120]{0:T(128)S(1)} %get-tuple-element.62), channel_id=1, source_target_pairs={{0,120},{8,0},{16,8},{24,16},{32,24},{40,32},{48,40},{56,48},{64,5... | collective-permute-start | bytes 1448 | tf_op jit(solution)/shard_map/ppermute | solution.py:106
  196.1 4.8 %collective-permute-done = f32[120]{0:T(128)S(1)} collective-permute-done((f32[120]{0:T(128)S(1)}, f32[120]{0:T(128)S(1)}, u32[]{:S(2)}, u32[]{:S(2)}) %collective-permute-start) | collective-permute-done | bytes 512 | tf_op jit(solution)/shard_map/ppermute | solution.py:104
  200.9 3.0 %collective-permute-start.9 = (f32[120]{0:T(128)S(1)}, f32[120]{0:T(128)S(1)}, u32[]{:S(2)}, u32[]{:S(2)}) collective-permute-start(f32[120]{0:T(128)S(1)} %collective-permute-done.8), channel_id=1, source_target_pairs={{0,120},{8,0},{16,8},{24,16},{32,24},{40,32},{48,40},{56,48},{64,5... | collective-permute-start | bytes 1448 | tf_op jit(solution)/shard_map/ppermute | solution.py:106
  205.1 2.9 %collective-permute-start.10 = (f32[120]{0:T(128)S(1)}, f32[120]{0:T(128)S(1)}, u32[]{:S(2)}, u32[]{:S(2)}) collective-permute-start(f32[120]{0:T(128)S(1)} %collective-permute-done.9), channel_id=1, source_target_pairs={{0,120},{8,0},{16,8},{24,16},{32,24},{40,32},{48,40},{56,48},{64,5... | collective-permute-start | bytes 1448 | tf_op jit(solution)/shard_map/ppermute | solution.py:106
  209.3 2.9 %collective-permute-start.11 = (f32[120]{0:T(128)S(1)}, f32[120]{0:T(128)S(1)}, u32[]{:S(2)}, u32[]{:S(2)}) collective-permute-start(f32[120]{0:T(128)S(1)} %collective-permute-done.10), channel_id=1, source_target_pairs={{0,120},{8,0},{16,8},{24,16},{32,24},{40,32},{48,40},{56,48},{64,5... | collective-permute-start | bytes 1448 | tf_op jit(solution)/shard_map/ppermute | solution.py:106
  213.5 2.9 %collective-permute-start.12 = (f32[120]{0:T(128)S(1)}, f32[120]{0:T(128)S(1)}, u32[]{:S(2)}, u32[]{:S(2)}) collective-permute-start(f32[120]{0:T(128)S(1)} %collective-permute-done.11), channel_id=1, source_target_pairs={{0,120},{8,0},{16,8},{24,16},{32,24},{40,32},{48,40},{56,48},{64,5... | collective-permute-start | bytes 1448 | tf_op jit(solution)/shard_map/ppermute | solution.py:106
  217.6 2.9 %collective-permute-start.13 = (f32[120]{0:T(128)S(1)}, f32[120]{0:T(128)S(1)}, u32[]{:S(2)}, u32[]{:S(2)}) collective-permute-start(f32[120]{0:T(128)S(1)} %collective-permute-done.12), channel_id=1, source_target_pairs={{0,120},{8,0},{16,8},{24,16},{32,24},{40,32},{48,40},{56,48},{64,5... | collective-permute-start | bytes 1448 | tf_op jit(solution)/shard_map/ppermute | solution.py:106
  221.8 2.9 %collective-permute-start.14 = (f32[120]{0:T(128)S(1)}, f32[120]{0:T(128)S(1)}, u32[]{:S(2)}, u32[]{:S(2)}) collective-permute-start(f32[120]{0:T(128)S(1)} %collective-permute-done.13), channel_id=1, source_target_pairs={{0,120},{8,0},{16,8},{24,16},{32,24},{40,32},{48,40},{56,48},{64,5... | collective-permute-start | bytes 1448 | tf_op jit(solution)/shard_map/ppermute | solution.py:106
  226.0 4.1 %collective-permute-done.7 = f32[120]{0:T(128)S(1)} collective-permute-done((f32[120]{0:T(128)S(1)}, f32[120]{0:T(128)S(1)}, u32[]{:S(2)}, u32[]{:S(2)}) %collective-permute-start.7) | collective-permute-done | bytes 512 | tf_op jit(solution)/shard_map/ppermute | solution.py:104
  233.8 2.5 reshape.153
  240.9 2.0 reshape.147
  (144 shorter events, 45.4 us)
Async XLA Ops:
  7.2 41.3 %copy-start = (f32[1,64,768]{2,1,0:T(8,128)S(1)}, f32[1,64,768]{2,1,0:T(8,128)}, u32[]{:S(2)}) copy-start(f32[1,64,768]{2,1,0:T(8,128)} %param.21) | copy-start | bytes 589828
  9.1 15.2 %all-to-all-start.2 = ((f32[16,1,1152]{2,1,0:T(1,128)}), f32[16,1,1152]{2,1,0:T(1,128)S(1)}, u32[]{:S(2)}, u32[]{:S(2)}) async-start(f32[16,1,1152]{2,1,0:T(1,128)} %reshape.148), calls=%async_computation.2 | async-start | bytes 147456 | tf_op jit(solution)/shard_map/all_to_all | solution.py:53
  24.3 11.4 %all-to-all-start = ((f32[16,1,1152]{2,1,0:T(1,128)}), f32[16,1,1152]{2,1,0:T(1,128)S(1)}, u32[]{:S(2)}, u32[]{:S(2)}) async-start(f32[16,1,1152]{2,1,0:T(1,128)} %reshape.144), calls=%async_computation | async-start | bytes 147456 | tf_op jit(solution)/shard_map/all_to_all | solution.py:52
  30.7 17.9 %copy-start.21 = (f32[1,1,251,64]{2,3,1,0:T(8,128)S(1)}, f32[1,1,251,64]{2,3,1,0:T(8,128)}, u32[]{:S(2)}) copy-start(f32[1,1,251,64]{2,3,1,0:T(8,128)} %param.20) | copy-start | bytes 192772
  35.7 11.8 %all-to-all-start.4 = ((f32[16,6,1,192]{3,2,1,0:T(1,128)}), f32[16,6,1,192]{3,2,1,0:T(1,128)S(1)}, u32[]{:S(2)}, u32[]{:S(2)}) async-start(f32[16,6,1,192]{3,2,1,0:T(1,128)} %bitcast.21), calls=%async_computation.4 | async-start | bytes 196608 | tf_op jit(solution)/shard_map/all_to_all | solution.py:54
  39.2 65.3 %all-reduce.3.cloned.1.call-start = ((), (), s32[]{:S(2)}) async-start(), calls=%async_computation.9 | async-start | bytes 491520 | tf_op jit(solution)/shard_map/psum | solution.py:79
  48.3 96.4 %reduce-scatter.2.cloned.1.call-start = ((), (), s32[]{:S(2)}) async-start(), calls=%async_computation.8 | async-start | bytes 983040 | tf_op jit(solution)/shard_map/reduce_scatter | solution.py:121
  123.2 14.8 %all-to-all-start.5 = ((f32[16,1,1152]{2,1,0:T(1,128)}), f32[16,1,1152]{2,1,0:T(1,128)S(1)}, u32[]{:S(2)}, u32[]{:S(2)}) async-start(f32[16,1,1152]{2,1,0:T(1,128)} %reshape.152), calls=%async_computation.5 | async-start | bytes 147456 | tf_op jit(solution)/shard_map/all_to_all | solution.py:92
  138.1 14.6 %all-to-all-start.3 = ((f32[16,1,1152]{2,1,0:T(1,128)}), f32[16,1,1152]{2,1,0:T(1,128)S(1)}, u32[]{:S(2)}, u32[]{:S(2)}) async-start(f32[16,1,1152]{2,1,0:T(1,128)} %reshape.150), calls=%async_computation.3 | async-start | bytes 147456 | tf_op jit(solution)/shard_map/all_to_all | solution.py:91
  145.7 46.9 %copy-start.22 = (f32[120]{0:T(128)S(1)}, f32[120]{0:T(128)}, u32[]{:S(2)}) copy-start(f32[120]{0:T(128)} %param.30) | copy-start | bytes 1444
  145.7 46.9 %copy-start.23 = (f32[120]{0:T(128)S(1)}, f32[120]{0:T(128)}, u32[]{:S(2)}) copy-start(f32[120]{0:T(128)} %param.25) | copy-start | bytes 1444
  145.7 85.2 %copy-start.2 = (f32[1,1,6,3072]{3,2,1,0:T(8,128)S(1)}, f32[1,1,6,3072]{3,2,1,0:T(8,128)}, u32[]{:S(2)}) copy-start(f32[1,1,6,3072]{3,2,1,0:T(8,128)} %get-tuple-element.55) | copy-start | bytes 221188
  145.7 85.9 %copy-start.5 = (f32[1,1,24,768]{3,2,1,0:T(8,128)S(1)}, f32[1,1,24,768]{3,2,1,0:T(8,128)}, u32[]{:S(2)}) copy-start(f32[1,1,24,768]{3,2,1,0:T(8,128)} %get-tuple-element.57) | copy-start | bytes 221188
  145.7 86.6 %copy-start.6 = (f32[1,1,24,768]{3,2,1,0:T(8,128)S(1)}, f32[1,1,24,768]{3,2,1,0:T(8,128)}, u32[]{:S(2)}) copy-start(f32[1,1,24,768]{3,2,1,0:T(8,128)} %get-tuple-element.59) | copy-start | bytes 221188
  152.6 80.4 %copy-start.3 = (f32[16,1,1152]{2,1,0:T(1,128)}, f32[16,1,1152]{2,1,0:T(1,128)S(1)}, u32[]{:S(2)}) copy-start(f32[16,1,1152]{2,1,0:T(1,128)S(1)} %all-to-all-done.3) | copy-start | bytes 221188
  152.6 21.8 %all-to-all-start.1 = ((f32[16,1,1152]{2,1,0:T(1,128)}), f32[16,1,1152]{2,1,0:T(1,128)S(1)}, u32[]{:S(2)}, u32[]{:S(2)}) async-start(f32[16,1,1152]{2,1,0:T(1,128)} %reshape.146), calls=%async_computation.1 | async-start | bytes 147456 | tf_op jit(solution)/shard_map/all_to_all | solution.py:90
  174.5 71.2 %all-to-all-start.6 = ((f32[251,16,48]{0,2,1:T(8,128)}), f32[251,16,48]{0,2,1:T(8,128)S(1)}, u32[]{:S(2)}, u32[]{:S(2)}) async-start(f32[251,16,48]{0,2,1:T(8,128)} %bitcast.34), calls=%async_computation.7 | async-start | bytes 1572864 | tf_op jit(solution)/shard_map/all_to_all | solution.py:126
  193.1 7.7 %collective-permute-start = (f32[120]{0:T(128)S(1)}, f32[120]{0:T(128)S(1)}, u32[]{:S(2)}, u32[]{:S(2)}) collective-permute-start(f32[120]{0:T(128)S(1)} %get-tuple-element.62), channel_id=1, source_target_pairs={{0,8},{8,16},{16,24},{24,32},{32,40},{40,48},{48,56},{56,64},{64,7... | collective-permute-start | bytes 1448 | tf_op jit(solution)/shard_map/ppermute | solution.py:104
  193.1 7.8 %collective-permute-start.8 = (f32[120]{0:T(128)S(1)}, f32[120]{0:T(128)S(1)}, u32[]{:S(2)}, u32[]{:S(2)}) collective-permute-start(f32[120]{0:T(128)S(1)} %get-tuple-element.62), channel_id=1, source_target_pairs={{0,120},{8,0},{16,8},{24,16},{32,24},{40,32},{48,40},{56,48},{64,5... | collective-permute-start | bytes 1448 | tf_op jit(solution)/shard_map/ppermute | solution.py:106
  200.9 4.2 %collective-permute-start.1 = (f32[120]{0:T(128)S(1)}, f32[120]{0:T(128)S(1)}, u32[]{:S(2)}, u32[]{:S(2)}) collective-permute-start(f32[120]{0:T(128)S(1)} %collective-permute-done), channel_id=1, source_target_pairs={{0,8},{8,16},{16,24},{24,32},{32,40},{40,48},{48,56},{56,64},{64,7... | collective-permute-start | bytes 1448 | tf_op jit(solution)/shard_map/ppermute | solution.py:104
  200.9 4.2 %collective-permute-start.9 = (f32[120]{0:T(128)S(1)}, f32[120]{0:T(128)S(1)}, u32[]{:S(2)}, u32[]{:S(2)}) collective-permute-start(f32[120]{0:T(128)S(1)} %collective-permute-done.8), channel_id=1, source_target_pairs={{0,120},{8,0},{16,8},{24,16},{32,24},{40,32},{48,40},{56,48},{64,5... | collective-permute-start | bytes 1448 | tf_op jit(solution)/shard_map/ppermute | solution.py:106
  205.0 4.2 %collective-permute-start.2 = (f32[120]{0:T(128)S(1)}, f32[120]{0:T(128)S(1)}, u32[]{:S(2)}, u32[]{:S(2)}) collective-permute-start(f32[120]{0:T(128)S(1)} %collective-permute-done.1), channel_id=1, source_target_pairs={{0,8},{8,16},{16,24},{24,32},{32,40},{40,48},{48,56},{56,64},{64,7... | collective-permute-start | bytes 1448 | tf_op jit(solution)/shard_map/ppermute | solution.py:104
  205.1 4.2 %collective-permute-start.10 = (f32[120]{0:T(128)S(1)}, f32[120]{0:T(128)S(1)}, u32[]{:S(2)}, u32[]{:S(2)}) collective-permute-start(f32[120]{0:T(128)S(1)} %collective-permute-done.9), channel_id=1, source_target_pairs={{0,120},{8,0},{16,8},{24,16},{32,24},{40,32},{48,40},{56,48},{64,5... | collective-permute-start | bytes 1448 | tf_op jit(solution)/shard_map/ppermute | solution.py:106
  209.2 4.2 %collective-permute-start.3 = (f32[120]{0:T(128)S(1)}, f32[120]{0:T(128)S(1)}, u32[]{:S(2)}, u32[]{:S(2)}) collective-permute-start(f32[120]{0:T(128)S(1)} %collective-permute-done.2), channel_id=1, source_target_pairs={{0,8},{8,16},{16,24},{24,32},{32,40},{40,48},{48,56},{56,64},{64,7... | collective-permute-start | bytes 1448 | tf_op jit(solution)/shard_map/ppermute | solution.py:104
  209.3 4.2 %collective-permute-start.11 = (f32[120]{0:T(128)S(1)}, f32[120]{0:T(128)S(1)}, u32[]{:S(2)}, u32[]{:S(2)}) collective-permute-start(f32[120]{0:T(128)S(1)} %collective-permute-done.10), channel_id=1, source_target_pairs={{0,120},{8,0},{16,8},{24,16},{32,24},{40,32},{48,40},{56,48},{64,5... | collective-permute-start | bytes 1448 | tf_op jit(solution)/shard_map/ppermute | solution.py:106
  213.4 4.2 %collective-permute-start.4 = (f32[120]{0:T(128)S(1)}, f32[120]{0:T(128)S(1)}, u32[]{:S(2)}, u32[]{:S(2)}) collective-permute-start(f32[120]{0:T(128)S(1)} %collective-permute-done.3), channel_id=1, source_target_pairs={{0,8},{8,16},{16,24},{24,32},{32,40},{40,48},{48,56},{56,64},{64,7... | collective-permute-start | bytes 1448 | tf_op jit(solution)/shard_map/ppermute | solution.py:104
  213.5 4.2 %collective-permute-start.12 = (f32[120]{0:T(128)S(1)}, f32[120]{0:T(128)S(1)}, u32[]{:S(2)}, u32[]{:S(2)}) collective-permute-start(f32[120]{0:T(128)S(1)} %collective-permute-done.11), channel_id=1, source_target_pairs={{0,120},{8,0},{16,8},{24,16},{32,24},{40,32},{48,40},{56,48},{64,5... | collective-permute-start | bytes 1448 | tf_op jit(solution)/shard_map/ppermute | solution.py:106
  217.6 4.2 %collective-permute-start.5 = (f32[120]{0:T(128)S(1)}, f32[120]{0:T(128)S(1)}, u32[]{:S(2)}, u32[]{:S(2)}) collective-permute-start(f32[120]{0:T(128)S(1)} %collective-permute-done.4), channel_id=1, source_target_pairs={{0,8},{8,16},{16,24},{24,32},{32,40},{40,48},{48,56},{56,64},{64,7... | collective-permute-start | bytes 1448 | tf_op jit(solution)/shard_map/ppermute | solution.py:104
  217.6 4.2 %collective-permute-start.13 = (f32[120]{0:T(128)S(1)}, f32[120]{0:T(128)S(1)}, u32[]{:S(2)}, u32[]{:S(2)}) collective-permute-start(f32[120]{0:T(128)S(1)} %collective-permute-done.12), channel_id=1, source_target_pairs={{0,120},{8,0},{16,8},{24,16},{32,24},{40,32},{48,40},{56,48},{64,5... | collective-permute-start | bytes 1448 | tf_op jit(solution)/shard_map/ppermute | solution.py:106
  221.7 4.2 %collective-permute-start.6 = (f32[120]{0:T(128)S(1)}, f32[120]{0:T(128)S(1)}, u32[]{:S(2)}, u32[]{:S(2)}) collective-permute-start(f32[120]{0:T(128)S(1)} %collective-permute-done.5), channel_id=1, source_target_pairs={{0,8},{8,16},{16,24},{24,32},{32,40},{40,48},{48,56},{56,64},{64,7... | collective-permute-start | bytes 1448 | tf_op jit(solution)/shard_map/ppermute | solution.py:104
  221.8 4.2 %collective-permute-start.14 = (f32[120]{0:T(128)S(1)}, f32[120]{0:T(128)S(1)}, u32[]{:S(2)}, u32[]{:S(2)}) collective-permute-start(f32[120]{0:T(128)S(1)} %collective-permute-done.13), channel_id=1, source_target_pairs={{0,120},{8,0},{16,8},{24,16},{32,24},{40,32},{48,40},{56,48},{64,5... | collective-permute-start | bytes 1448 | tf_op jit(solution)/shard_map/ppermute | solution.py:106
  225.9 4.2 %collective-permute-start.7 = (f32[120]{0:T(128)S(1)}, f32[120]{0:T(128)S(1)}, u32[]{:S(2)}, u32[]{:S(2)}) collective-permute-start(f32[120]{0:T(128)S(1)} %collective-permute-done.6), channel_id=1, source_target_pairs={{0,8},{8,16},{16,24},{24,32},{32,40},{40,48},{48,56},{56,64},{64,7... | collective-permute-start | bytes 1448 | tf_op jit(solution)/shard_map/ppermute | solution.py:104
  (16 other events, 139.6 us)
Sparse Core Ops, SparseCore 0:
  48.4 56.0 all-reduce.2
  108.1 30.1 reduce-scatter.1
